TPU v7x, 512 devices: a whole 4x4x16 slice. The times are simulated.
512 devices in a mesh: row: 16 (over y, x), col: 32 (over z, core).
Axes of the slice: x: 4, y: 4, z: 16, core: 2. Of those that a mesh axis runs over, the one named last changes fastest.
Arguments:
- residual_in: float32 [8, 16, 128, 256], P(None, 'row', None, 'col'), may hold values from -6 to 6
- diag_inverse: bfloat16 [8, 16, 256, 256], P(None, 'row'), may hold values from -0.04 to 1.04, as said below
- lower_blocks: bfloat16 [7, 16, 3, 256, 256], P(None, 'row'), may hold values from -0.15625 to 0.15625
- column_lists: int32 [7, 16, 3], replicated, may hold values from 0 to 111, as said below
Outputs:
- precond: float32 [8, 16, 128, 256], P(None, 'row', None, 'col')
Inputs may be any that keep to these rules, and one draw needn't show every extreme that they name: `column_lists`: for a block row of level s, every entry names a block row of a level below s; its first entry names a block row of level s - 1, and every block row of level s - 1 is named so by exactly one block row of level s. `diag_inverse`: each block is the identity plus small entries.
All inputs are finite; a program needn't handle non-finite values.
Results may differ from a plain program's by a relative error of at most 0.0003.
Values sent between devices are 32-bit elements; how exact they have to be, the bound alone decides.
A program may use at most 64 MiB of HBM per device.

v0:
```python
import jax
import jax.numpy as jnp
from jax import lax
from jax.sharding import PartitionSpec as P


def pick_index(array, index, axis_number):
    return lax.dynamic_index_in_dim(array, index, axis_number, keepdims=False)


def shards(residual_in, diag_inverse, lower_blocks, column_lists):
    highest = lax.Precision.HIGHEST
    sweep_input = lax.all_to_all(residual_in, "col", split_axis=2, concat_axis=3, tiled=True)[:, 0]
    slot_count, probe_count, block_size = sweep_input.shape
    owners = lax.axis_size("row")
    self_row = lax.axis_index("row")
    inverses = diag_inverse[:, 0]
    lowers = lower_blocks[:, 0]
    slot_numbers = jnp.arange(slot_count, dtype=jnp.int32)

    def solve_forward(current, source):
        inverse_block = pick_index(inverses, current, 0).astype(jnp.float32)
        return jnp.einsum("pc,dc->pd", source, inverse_block, precision=highest)

    def solve_backward(current, source):
        inverse_block = pick_index(inverses, current, 0).astype(jnp.float32)
        return jnp.einsum("pc,cd->pd", source, inverse_block, precision=highest)

    def contributions_of(current, solved):
        factor_blocks = pick_index(lowers, current - 1, 0).astype(jnp.float32)
        return jnp.einsum("pd,kdc->kpc", solved, factor_blocks, precision=highest)

    finished = jnp.zeros((slot_count, owners, probe_count, block_size), jnp.float32)
    forward = jnp.zeros((slot_count, probe_count, block_size), jnp.float32)
    forward = forward.at[0].set(solve_forward(0, sweep_input[0]))

    def forward_step(current, loop_state):
        finished, forward = loop_state
        previous = lax.dynamic_index_in_dim(forward, current - 1, 0, keepdims=True)
        arrived = lax.all_gather(previous, "row", axis=0, tiled=True)
        finished = lax.dynamic_update_index_in_dim(finished, arrived, current - 1, 0)
        targets = pick_index(pick_index(column_lists, current - 1, 0), self_row, 0)
        pulled = finished.reshape(slot_count * owners, probe_count, block_size)[targets]
        factor_blocks = pick_index(lowers, current - 1, 0).astype(jnp.float32)
        source = pick_index(sweep_input, current, 0) - jnp.einsum(
            "kpc,kdc->pd", pulled, factor_blocks, precision=highest
        )
        forward = lax.dynamic_update_index_in_dim(
            forward, solve_forward(current, source), current, 0
        )
        return (finished, forward)

    finished, forward = lax.fori_loop(1, slot_count, forward_step, (finished, forward))
    final_level = slot_count - 1
    backward = jnp.zeros((slot_count, probe_count, block_size), jnp.float32)
    backward = backward.at[final_level].set(solve_backward(final_level, forward[final_level]))

    def backward_step(counter, loop_state):
        accumulated, backward = loop_state
        current = final_level - counter
        contributions = contributions_of(current, pick_index(backward, current, 0))
        arrived = lax.all_gather(contributions[None], "row", axis=0, tiled=True)
        targets = pick_index(column_lists, current - 1, 0)
        owner_match = (targets % owners == self_row)[:, :, None]
        slot_match = (targets // owners)[:, :, None] == slot_numbers[None, None, :]
        routing = (owner_match & slot_match).astype(jnp.float32)
        accumulated = accumulated + jnp.einsum("nks,nkpc->spc", routing, arrived, precision=highest)
        source = pick_index(forward, current - 1, 0) - pick_index(accumulated, current - 1, 0)
        backward = lax.dynamic_update_index_in_dim(
            backward, solve_backward(current - 1, source), current - 1, 0
        )
        return (accumulated, backward)

    accumulated = jnp.zeros((slot_count, probe_count, block_size), jnp.float32)
    accumulated, backward = lax.fori_loop(0, final_level, backward_step, (accumulated, backward))
    return lax.all_to_all(backward[:, None], "col", split_axis=3, concat_axis=2, tiled=True)


def solution(mesh):
    placed = (
        P(None, "row", None, "col"),
        P(None, "row", None, None),
        P(None, "row", None, None, None),
        P(),
    )
    return jax.shard_map(
        shards, mesh=mesh, in_specs=placed, out_specs=P(None, "row", None, "col"), check_vma=False
    )
```

profile of v0, /device:TPU:1, one launch (start us, length us, event | category | flops | bytes accessed | tf_op | source)
XLA Modules:
  0.0 401.5 jit_solution(119904311457603688)
XLA Ops:
  2.0 16.7 %all-to-all-start = ((f32[32,1,256]{2,1,0:T(1,128)}), f32[32,1,256]{2,1,0:T(1,128)S(1)}, u32[]{:S(2)}, u32[]{:S(2)}) async-start(f32[32,1,256]{2,1,0:T(1,128)} %reshape.230), calls=%async_computation | async-start | bytes 65536 | tf_op jit(solution)/shard_map/all_to_all | solution.py:13
  19.6 11.3 %all-to-all-done = f32[32,1,256]{2,1,0:T(1,128)S(1)} async-done(((f32[32,1,256]{2,1,0:T(1,128)}), f32[32,1,256]{2,1,0:T(1,128)S(1)}, u32[]{:S(2)}, u32[]{:S(2)}) %all-to-all-start) | async-done | bytes 32800 | tf_op jit(solution)/shard_map/all_to_all | solution.py:13
  33.5 135.3 %while.44 = (s32[]{:T(128)}, f32[8,16,4,256]{3,2,1,0:T(4,128)S(1)}, f32[8,4,256]{2,1,0:T(4,128)S(1)}, f32[8,4,256]{2,1,0:T(4,128)S(1)}, s32[7,16,3]{2,1,0:T(8,12...) while((s32[]{:T(128)}, f32[8,16,4,256]{3,2,1,0:T(4,128)S(1)}, ...), condition=%wide.region_1.2_spmd, body=%wide.region_0.1_spmd.sunk | while | flops 12584975 | bytes 792307 | solution.py:53
  33.6 18.4 %all_gather.31 = f32[16,4,256]{2,1,0:T(4,128)S(1)} all-gather(f32[1,4,256]{2,1,0:T(4,128)S(1)} %constant_dynamic-slice_fusion.7), channel_id=1, replica_groups=mesh['row'=16,'col'=32] {'row'}, dimensions={0}, use_global_device_ids=true | all-gather | bytes 69632 | tf_op jit(solution)/shard_map/while/body/eval_jaxpr/all_gather | solution.py:40
  52.6 1.4 fusion.65
  54.3 17.9 %all_gather.31 = f32[16,4,256]{2,1,0:T(4,128)S(1)} all-gather(f32[1,4,256]{2,1,0:T(4,128)S(1)} %constant_dynamic-slice_fusion.7), channel_id=1, replica_groups=mesh['row'=16,'col'=32] {'row'}, dimensions={0}, use_global_device_ids=true | all-gather | bytes 69632 | tf_op jit(solution)/shard_map/while/body/eval_jaxpr/all_gather | solution.py:40
  72.9 1.4 fusion.65
  74.5 15.6 %all_gather.31 = f32[16,4,256]{2,1,0:T(4,128)S(1)} all-gather(f32[1,4,256]{2,1,0:T(4,128)S(1)} %constant_dynamic-slice_fusion.7), channel_id=1, replica_groups=mesh['row'=16,'col'=32] {'row'}, dimensions={0}, use_global_device_ids=true | all-gather | bytes 69632 | tf_op jit(solution)/shard_map/while/body/eval_jaxpr/all_gather | solution.py:40
  90.7 1.4 fusion.65
  92.4 18.1 %all_gather.31 = f32[16,4,256]{2,1,0:T(4,128)S(1)} all-gather(f32[1,4,256]{2,1,0:T(4,128)S(1)} %constant_dynamic-slice_fusion.7), channel_id=1, replica_groups=mesh['row'=16,'col'=32] {'row'}, dimensions={0}, use_global_device_ids=true | all-gather | bytes 69632 | tf_op jit(solution)/shard_map/while/body/eval_jaxpr/all_gather | solution.py:40
  111.1 1.4 fusion.65
  112.7 15.4 %all_gather.31 = f32[16,4,256]{2,1,0:T(4,128)S(1)} all-gather(f32[1,4,256]{2,1,0:T(4,128)S(1)} %constant_dynamic-slice_fusion.7), channel_id=1, replica_groups=mesh['row'=16,'col'=32] {'row'}, dimensions={0}, use_global_device_ids=true | all-gather | bytes 69632 | tf_op jit(solution)/shard_map/while/body/eval_jaxpr/all_gather | solution.py:40
  128.8 1.4 fusion.65
  130.5 18.4 %all_gather.31 = f32[16,4,256]{2,1,0:T(4,128)S(1)} all-gather(f32[1,4,256]{2,1,0:T(4,128)S(1)} %constant_dynamic-slice_fusion.7), channel_id=1, replica_groups=mesh['row'=16,'col'=32] {'row'}, dimensions={0}, use_global_device_ids=true | all-gather | bytes 69632 | tf_op jit(solution)/shard_map/while/body/eval_jaxpr/all_gather | solution.py:40
  151.1 15.4 %all_gather.31 = f32[16,4,256]{2,1,0:T(4,128)S(1)} all-gather(f32[1,4,256]{2,1,0:T(4,128)S(1)} %constant_dynamic-slice_fusion.7), channel_id=1, replica_groups=mesh['row'=16,'col'=32] {'row'}, dimensions={0}, use_global_device_ids=true | all-gather | bytes 69632 | tf_op jit(solution)/shard_map/while/body/eval_jaxpr/all_gather | solution.py:40
  169.1 137.8 %while.45 = (s32[]{:T(128)}, f32[8,4,256]{2,0,1:T(8,128)S(1)}, f32[8,4,256]{2,1,0:T(4,128)S(1)}, s32[7,16,3]{1,0,2:T(8,128)}, s32[]{:T(128)}, /*index=5*/bf16[7,...) while((s32[]{:T(128)}, f32[8,4,256]{2,0,1:T(8,128)S(1)}, ...), condition=%wide.region_3.4_spmd.clone, body=%wide.region_2.3_spmd.clone.sunk | while | flops 17320988 | bytes 1042948 | solution.py:75
  170.4 18.4 %all-gather.3 = f32[48,4,256]{2,1,0:T(4,128)S(1)} all-gather(f32[3,4,256]{2,1,0:T(4,128)S(1)} %convolution_bitcast_fusion.8), channel_id=2, replica_groups=mesh['row'=16,'col'=32] {'row'}, dimensions={0}, use_global_device_ids=true | all-gather | bytes 208896 | tf_op jit(solution)/shard_map/while/body/eval_jaxpr/all_gather | solution.py:62
  191.2 15.8 %all-gather.3 = f32[48,4,256]{2,1,0:T(4,128)S(1)} all-gather(f32[3,4,256]{2,1,0:T(4,128)S(1)} %convolution_bitcast_fusion.8), channel_id=2, replica_groups=mesh['row'=16,'col'=32] {'row'}, dimensions={0}, use_global_device_ids=true | all-gather | bytes 208896 | tf_op jit(solution)/shard_map/while/body/eval_jaxpr/all_gather | solution.py:62
  209.5 18.2 %all-gather.3 = f32[48,4,256]{2,1,0:T(4,128)S(1)} all-gather(f32[3,4,256]{2,1,0:T(4,128)S(1)} %convolution_bitcast_fusion.8), channel_id=2, replica_groups=mesh['row'=16,'col'=32] {'row'}, dimensions={0}, use_global_device_ids=true | all-gather | bytes 208896 | tf_op jit(solution)/shard_map/while/body/eval_jaxpr/all_gather | solution.py:62
  230.2 15.7 %all-gather.3 = f32[48,4,256]{2,1,0:T(4,128)S(1)} all-gather(f32[3,4,256]{2,1,0:T(4,128)S(1)} %convolution_bitcast_fusion.8), channel_id=2, replica_groups=mesh['row'=16,'col'=32] {'row'}, dimensions={0}, use_global_device_ids=true | all-gather | bytes 208896 | tf_op jit(solution)/shard_map/while/body/eval_jaxpr/all_gather | solution.py:62
  248.3 18.0 %all-gather.3 = f32[48,4,256]{2,1,0:T(4,128)S(1)} all-gather(f32[3,4,256]{2,1,0:T(4,128)S(1)} %convolution_bitcast_fusion.8), channel_id=2, replica_groups=mesh['row'=16,'col'=32] {'row'}, dimensions={0}, use_global_device_ids=true | all-gather | bytes 208896 | tf_op jit(solution)/shard_map/while/body/eval_jaxpr/all_gather | solution.py:62
  268.8 15.7 %all-gather.3 = f32[48,4,256]{2,1,0:T(4,128)S(1)} all-gather(f32[3,4,256]{2,1,0:T(4,128)S(1)} %convolution_bitcast_fusion.8), channel_id=2, replica_groups=mesh['row'=16,'col'=32] {'row'}, dimensions={0}, use_global_device_ids=true | all-gather | bytes 208896 | tf_op jit(solution)/shard_map/while/body/eval_jaxpr/all_gather | solution.py:62
  287.0 18.7 %all-gather.3 = f32[48,4,256]{2,1,0:T(4,128)S(1)} all-gather(f32[3,4,256]{2,1,0:T(4,128)S(1)} %convolution_bitcast_fusion.8), channel_id=2, replica_groups=mesh['row'=16,'col'=32] {'row'}, dimensions={0}, use_global_device_ids=true | all-gather | bytes 208896 | tf_op jit(solution)/shard_map/while/body/eval_jaxpr/all_gather | solution.py:62
  307.7 90.9 %all_to_all.33 = f32[32,1,256]{2,1,0:T(1,128)S(1)} all-to-all(f32[32,1,256]{2,1,0:T(1,128)S(1)} %reshape.232), channel_id=1, replica_groups=mesh['row'=16,'col'=32] {'col'}, dimensions={0} | all-to-all | bytes 65536 | tf_op jit(solution)/shard_map/all_to_all | solution.py:76
  (127 shorter events, 35.4 us)
Async XLA Ops:
  0.0 33.2 %copy-start = (bf16[8,1,256,256]{3,2,1,0:T(8,128)(2,1)S(1)}, bf16[8,1,256,256]{3,2,1,0:T(8,128)(2,1)}, u32[]{:S(2)}) copy-start(bf16[8,1,256,256]{3,2,1,0:T(8,128)(2,1)} %param.13) | copy-start | bytes 3145732
  2.0 28.9 %all-to-all-start = ((f32[32,1,256]{2,1,0:T(1,128)}), f32[32,1,256]{2,1,0:T(1,128)S(1)}, u32[]{:S(2)}, u32[]{:S(2)}) async-start(f32[32,1,256]{2,1,0:T(1,128)} %reshape.230), calls=%async_computation | async-start | bytes 65536 | tf_op jit(solution)/shard_map/all_to_all | solution.py:13
where the time goes:
time: 403 us; the launch traced here: 402 us
  blocking collectives  331 us (82%)
  matrix products  23.7 us (6%)
  local copies, waits for them, and re-layouts  16.8 us (4%)
  starting transfers between devices  16.7 us (4%)
  waiting for transfers between devices  11.3 us (3%)
    all_gather x7, blocking collectives, backward_step(): arrived = lax.all_gather(contributions[None], 'row', axis=0, tiled=True)  120 us
    all_gather x7, blocking collectives, forward_step(): arrived = lax.all_gather(previous, 'row', axis=0, tiled=True)  119 us
    all_to_all x1, blocking collectives, shards(): lax.all_to_all(backward[:, None], 'col', split_axis=3, concat_axis=2, til...  90.9 us
    all_to_all x1, starting transfers between devices, shards(): lax.all_to_all(residual_in, 'col', split_axis=2, concat_axis=3, tiled=True)  16.7 us
    all_to_all x1, waiting for transfers between devices, shards(): lax.all_to_all(residual_in, 'col', split_axis=2, concat_axis=3, tiled=True)  11.3 us
    dot_general x7, matrix products, forward_step(): jnp.einsum('kpc,kdc->pd', pulled, factor_blocks, precision=highest)  9.65 us
    dot_general x7, matrix products, contributions_of(): return jnp.einsum('pd,kdc->kpc', solved, factor_blocks, precision=highest)  9.17 us
  transfers between devices with their start and end apart: 1, of which 1 were waited for; matrix products, arithmetic and copies ran while one was open for 0% of the time, Pallas kernels for 0%

commit v1 on v0

v1 whole, which is shorter than its diff:
```python
import functools

import jax
import jax.numpy as jnp
from jax import lax
from jax.experimental import pallas as pl
from jax.experimental.pallas import tpu as pltpu
from jax.sharding import PartitionSpec as P

MESH = pl.DeviceIdType.MESH
NT = (((1,), (1,)), ((), ()))
NN = (((1,), (0,)), ((), ()))


def split(packed):
    first = lax.broadcasted_iota(jnp.int32, packed.shape, 0) < 4
    wide = jnp.concatenate([jnp.where(first, packed, 0.0), jnp.where(first, 0.0, packed)], axis=1)
    high = wide.astype(jnp.bfloat16).astype(jnp.float32)
    return jnp.concatenate([high, wide - high], axis=0).astype(jnp.bfloat16)


def merge(product):
    both = product[:8] + product[8:]
    left, right = both[:, :128], both[:, 128:]
    left = left + pltpu.roll(left, 4, 0)
    right = right + pltpu.roll(right, 4, 0)
    first = lax.broadcasted_iota(jnp.int32, left.shape, 0) < 4
    return jnp.where(first, left, right)


def times(rows, block, dims):
    return lax.dot_general(rows, block, dims, preferred_element_type=jnp.float32)


def kernel(levels, n, own_ref, r_ref, d_ref, l_ref, out_ref, mine, came, done, part, base, give, back,
           fsend, frecv, bsend, brecv):
    me = lax.axis_index("row")
    peers = [lax.rem(me + j, n) for j in range(1, n)]
    barrier = pltpu.get_barrier_semaphore()
    for peer in peers:
        pl.semaphore_signal(barrier, inc=1, device_id={"row": peer}, device_id_type=MESH)
    pl.semaphore_wait(barrier, n - 1)

    mine[0] = merge(times(split(r_ref[0]), d_ref[0], NT))

    def forward(level, carry):
        last = level - 1
        for j, peer in enumerate(peers):
            pltpu.make_async_remote_copy(
                mine.at[last], came.at[last, j], fsend.at[last], frecv.at[last],
                device_id={"row": peer}, device_id_type=MESH).start()
        done[last * n + me] = mine[last]
        pltpu.make_async_copy(came.at[last], came.at[last], frecv.at[last]).wait()
        for j in range(1, n):
            done[last * n + lax.rem(me - j + n, n)] = came[last, j - 1]
        total = None
        for k in range(3):
            term = times(split(done[own_ref[last, k]]), l_ref[last, k], NT)
            total = term if total is None else total + term
        mine[level] = merge(times(split(r_ref[level] - merge(total)), d_ref[level], NT))
        return carry

    lax.fori_loop(1, levels, forward, 0)
    top = levels - 1
    out_ref[top] = merge(times(split(mine[top]), d_ref[top], NN))
    base[...] = jnp.zeros_like(base)

    def backward(step, carry):
        level = top - step
        low = level - 1
        rows = split(out_ref[level])
        news = [merge(times(rows, l_ref[low, k], NN)) for k in range(3)]
        for k in range(3):
            part[low, k] = news[k]
        wants = [jnp.full((8, 128), own_ref[low, k] - low * n, jnp.int32) for k in range(3)]
        for r in range(n):
            message = base[r]
            for k in range(3):
                message = message + jnp.where(wants[k] == r, news[k], 0.0)
            give[low, r] = message
        for j, peer in enumerate(peers):
            pltpu.make_async_remote_copy(
                give.at[low, peer], back.at[low, j], bsend.at[low], brecv.at[low],
                device_id={"row": peer}, device_id_type=MESH).start()
        own = give[low, me]

        base[...] = jnp.zeros_like(base)

        def older(source, carry):
            for k in range(1, 3):
                want = jnp.full((8, 128), own_ref[source, k] - (low - 1) * n, jnp.int32)
                value = part[source, k]
                for r in range(n):
                    base[r] = base[r] + jnp.where(want == r, value, 0.0)
            return carry

        lax.fori_loop(low, top, older, 0)
        pltpu.make_async_copy(back.at[low], back.at[low], brecv.at[low]).wait()
        for j in range(n - 1):
            own = own + back[low, j]
        out_ref[low] = merge(times(split(mine[low] - own), d_ref[low], NN))
        return carry

    lax.fori_loop(0, top, backward, 0)

    def drain(level, carry):
        pltpu.make_async_copy(came.at[level], came.at[level], fsend.at[level]).wait()
        pltpu.make_async_copy(back.at[level], back.at[level], bsend.at[level]).wait()
        return carry

    lax.fori_loop(0, top, drain, 0)


def shards(residual_in, diag_inverse, lower_blocks, column_lists):
    sweep_input = lax.all_to_all(residual_in, "col", split_axis=2, concat_axis=3, tiled=True)[:, 0]
    levels, probes, cells = sweep_input.shape
    n = lax.axis_size("row")
    packed = sweep_input.reshape(levels, probes, 2, 128).transpose(0, 2, 1, 3).reshape(levels, 8, 128)
    own = lax.dynamic_index_in_dim(column_lists, lax.axis_index("row"), 1, keepdims=False)
    vmem = pl.BlockSpec(memory_space=pltpu.VMEM)
    f32 = jnp.float32
    solved = pl.pallas_call(
        functools.partial(kernel, levels, n),
        out_shape=jax.ShapeDtypeStruct((levels, 8, 128), f32),
        in_specs=[pl.BlockSpec(memory_space=pltpu.SMEM), vmem, vmem, vmem],
        out_specs=vmem,
        scratch_shapes=[
            pltpu.VMEM((levels, 8, 128), f32),
            pltpu.VMEM((levels - 1, n - 1, 8, 128), f32),
            pltpu.VMEM(((levels - 1) * n, 8, 128), f32),
            pltpu.VMEM((levels - 1, 3, 8, 128), f32),
            pltpu.VMEM((n, 8, 128), f32),
            pltpu.VMEM((levels - 1, n, 8, 128), f32),
            pltpu.VMEM((levels - 1, n - 1, 8, 128), f32),
            pltpu.SemaphoreType.DMA((levels - 1,)),
            pltpu.SemaphoreType.DMA((levels - 1,)),
            pltpu.SemaphoreType.DMA((levels - 1,)),
            pltpu.SemaphoreType.DMA((levels - 1,)),
        ],
        compiler_params=pltpu.CompilerParams(
            collective_id=0, has_side_effects=True, vmem_limit_bytes=32 * 1024 * 1024),
    )(own, packed, diag_inverse[:, 0], lower_blocks[:, 0])
    backward = solved.reshape(levels, 2, probes, 128).transpose(0, 2, 1, 3).reshape(levels, probes, cells)
    return lax.all_to_all(backward[:, None], "col", split_axis=3, concat_axis=2, tiled=True)


def solution(mesh):
    placed = (
        P(None, "row", None, "col"),
        P(None, "row", None, None),
        P(None, "row", None, None, None),
        P(),
    )
    return jax.shard_map(
        shards, mesh=mesh, in_specs=placed, out_specs=P(None, "row", None, "col"), check_vma=False
    )
```

time: 403 us -> 135 us (0.33)
  blocking collectives: 331 us -> 28.6 us
  Pallas kernels: 0 us -> 66.6 us
  matrix products: 23.7 us -> 0 us
  local copies, waits for them, and re-layouts: 16.8 us -> 9.68 us
    all_gather x14 -> x0, blocking collectives: 240 us -> none  [the longest x7 120 us: backward_step(): arrived = lax.all_gather(contributions[None], 'row', axis=0, tiled=True)]
    pallas_call x0 -> x1, Pallas kernels: none -> 66.6 us  [shards(): pl.pallas_call(functools.partial(kernel, levels, n), out_shape=jax.ShapeD...]
    all_to_all x1, blocking collectives: 90.9 us -> 28.6 us  [shards(): lax.all_to_all(backward[:, None], 'col', split_axis=3, concat_axis=2, til...]
    dot_general x37 -> x0, matrix products: 23.7 us -> none  [the longest x7 9.65 us: forward_step(): jnp.einsum('kpc,kdc->pd', pulled, factor_blocks, precision=highest)]
    dynamic_slice x21 -> x1, local copies, waits for them, and re-layouts: 5.09 us -> 0.07 us  [shards(): lax.dynamic_index_in_dim(column_lists, lax.axis_index('row'), 1, keepdims...]
where the time goes in v1:
time: 135 us
  Pallas kernels  66.6 us (49%)
  blocking collectives  28.6 us (21%)
  starting transfers between devices  16.8 us (12%)
  waiting for transfers between devices  11.9 us (9%)
  local copies, waits for them, and re-layouts  9.68 us (7%)
  other arithmetic  1.44 us (1%)
    pallas_call x1, Pallas kernels, shards(): pl.pallas_call(functools.partial(kernel, levels, n), out_shape=jax.ShapeD...  66.6 us
    all_to_all x1, blocking collectives, shards(): lax.all_to_all(backward[:, None], 'col', split_axis=3, concat_axis=2, til...  28.6 us
    all_to_all x1, starting transfers between devices, shards(): lax.all_to_all(residual_in, 'col', split_axis=2, concat_axis=3, tiled=True)  16.8 us
    all_to_all x1, waiting for transfers between devices, shards(): lax.all_to_all(residual_in, 'col', split_axis=2, concat_axis=3, tiled=True)  11.9 us
    unnamed x11, local copies, waits for them, and re-layouts  4.76 us
  transfers between devices with their start and end apart: 1, of which 1 were waited for; matrix products, arithmetic and copies ran while one was open for 0% of the time, Pallas kernels for 0%

profile of v1, /device:TPU:1, one launch (start us, length us, event | category | flops | bytes accessed | tf_op | source)
XLA Modules:
  0.0 135.1 jit_solution(15122136549822128373)
XLA Ops:
  0.0 0.0 copy-start
  0.0 1.1 copy.21
  1.2 0.9 reshape.9
  2.1 16.8 %all-to-all-start = ((f32[32,1,256]{2,1,0:T(1,128)}), f32[32,1,256]{2,1,0:T(1,128)S(1)}, u32[]{:S(2)}, u32[]{:S(2)}) async-start(f32[32,1,256]{2,1,0:T(1,128)} %reshape.9), calls=%async_computation | async-start | bytes 65536 | tf_op jit(solution)/shard_map/all_to_all | solution.py:115
  18.8 0.0 copy-done
  18.8 0.1 constant_dynamic-slice_fusion
  18.9 0.1 copy.29
  19.0 11.9 %all-to-all-done = f32[32,1,256]{2,1,0:T(1,128)S(1)} async-done(((f32[32,1,256]{2,1,0:T(1,128)}), f32[32,1,256]{2,1,0:T(1,128)S(1)}, u32[]{:S(2)}, u32[]{:S(2)}) %all-to-all-start) | async-done | bytes 32800 | tf_op jit(solution)/shard_map/all_to_all | solution.py:115
  30.9 0.5 broadcast
  31.4 0.7 reduce
  32.2 0.3 reshape.10
  32.5 1.1 copy.22
  33.6 1.3 reshape_squeeze.3
  34.9 0.0 copy-start.2
  34.9 1.2 copy-done.2
  36.2 66.6 %shard_map.46 = f32[8,8,128]{2,1,0:T(8,128)S(1)} custom-call(s32[7,3]{1,0:T(8,128)S(1)} %bitcast.27, f32[8,8,128]{2,1,0:T(8,128)S(1)} %bitcast.26, bf16[8,256,256]{2,1,0:T(8,128)(2,1)S(1)} %bitcast.24, bf16[7,3,256,256]{3,2,1,0:T(8,128)(2,1)S(1)} %bitcast.23), custom_call_target="tpu_custom_call" | custom-call | tf_op jit(solution)/shard_map/pallas_call | solution.py:122
  102.8 0.2 copy.25
  103.0 0.5 reshape.11
  103.5 28.6 %all_to_all.33 = f32[32,1,256]{2,1,0:T(1,128)S(1)} all-to-all(f32[32,1,256]{2,1,0:T(1,128)S(1)} %reshape.11), channel_id=1, replica_groups=mesh['row'=16,'col'=32] {'col'}, dimensions={0} | all-to-all | bytes 65536 | tf_op jit(solution)/shard_map/all_to_all | solution.py:144
  132.2 0.7 reduce.1
  132.9 0.7 reshape.12
  133.6 0.4 copy.30
  134.0 0.3 copy.27
  134.3 0.8 copy.28
  (3 shorter events, 0.0 us)
Async XLA Ops:
  0.0 18.8 %copy-start = (s32[7,16,3]{1,0,2:T(8,128)S(1)}, s32[7,16,3]{1,0,2:T(8,128)}, u32[]{:S(2)}) copy-start(s32[7,16,3]{1,0,2:T(8,128)} %param.7) | copy-start | bytes 4036
  0.0 34.9 %copy-start.1 = (bf16[7,1,3,256,256]{4,3,2,1,0:T(8,128)(2,1)S(1)}, bf16[7,1,3,256,256]{4,3,2,1,0:T(8,128)(2,1)}, u32[]{:S(2)}) copy-start(bf16[7,1,3,256,256]{4,3,2,1,0:T(8,128)(2,1)} %param.6) | copy-start | bytes 8257540
  2.1 28.9 %all-to-all-start = ((f32[32,1,256]{2,1,0:T(1,128)}), f32[32,1,256]{2,1,0:T(1,128)S(1)}, u32[]{:S(2)}, u32[]{:S(2)}) async-start(f32[32,1,256]{2,1,0:T(1,128)} %reshape.9), calls=%async_computation | async-start | bytes 65536 | tf_op jit(solution)/shard_map/all_to_all | solution.py:115
  34.9 1.2 copy-start.2
